TPU v7x, 32 devices: a whole 2x2x4 slice. The times are simulated.
32 devices in a mesh: dp: 8 (over z, core), tensor: 4 (over y, x).
Axes of the slice: x: 2, y: 2, z: 4, core: 2. Of those that a mesh axis runs over, the one named last changes fastest.
Arguments:
- tokens: bfloat16 [16, 512, 2048], P('dp', 'tensor'), may hold values from -6 to 6
- cotangent: bfloat16 [16, 512, 2048], P('dp', 'tensor'), may hold values from -6 to 6
- lengths: int32 [16], P('dp'), may hold values from 1 to 512, 5120 in all
- attn_gain: float32 [2048], replicated, may hold values from 0.5 to 1.5
- mlp_gain: float32 [2048], replicated, may hold values from 0.5 to 1.5
- w_query: float32 [2048, 2048], P('dp', 'tensor'), may hold values from -0.125 to 0.125
- w_keyval: float32 [2, 2048, 512], P(None, 'dp', 'tensor'), may hold values from -0.125 to 0.125
- w_output: float32 [2048, 2048], P('tensor', 'dp'), may hold values from -1 to 1
- w_gateup: float32 [2, 2048, 8192], P(None, 'dp', 'tensor'), may hold values from -0.125 to 0.125
- w_down: float32 [8192, 2048], P('tensor', 'dp'), may hold values from -0.0625 to 0.0625
- m_attn_gain: float32 [2048], replicated, may hold values from -128 to 128
- m_mlp_gain: float32 [2048], replicated, may hold values from -48 to 48
- m_query: float32 [2048, 2048], P('dp', 'tensor'), may hold values from -96 to 96
- m_keyval: float32 [2, 2048, 512], P(None, 'dp', 'tensor'), may hold values from -128 to 128
- m_output: float32 [2048, 2048], P('tensor', 'dp'), may hold values from -6 to 6
- m_gateup: float32 [2, 2048, 8192], P(None, 'dp', 'tensor'), may hold values from -16 to 16
- m_down: float32 [8192, 2048], P('tensor', 'dp'), may hold values from -48 to 48
- s_attn_gain: float32 [2048], replicated, may hold values from 21.2992 to 335.872
- s_mlp_gain: float32 [2048], replicated, may hold values from 2.359296 to 37.35552
- s_query: float32 [2048, 2048], P('dp', 'tensor'), may hold values from 8.68352 to 137.6256
- s_keyval: float32 [2, 2048, 512], P(None, 'dp', 'tensor'), may hold values from 22.9376 to 360.448
- s_output: float32 [2048, 2048], P('tensor', 'dp'), may hold values from 0.196608 to 3.11296
- s_gateup: float32 [2, 2048, 8192], P(None, 'dp', 'tensor'), may hold values from 0.26624 to 4.3008
- s_down: float32 [8192, 2048], P('tensor', 'dp'), may hold values from 2.12992 to 33.5872
Outputs:
- output: bfloat16 [16, 512, 2048], P('dp', 'tensor')
- input_grad: float32 [16, 512, 2048], P('dp', 'tensor')
- grad_attn_gain: float32 [2048], replicated
- grad_mlp_gain: float32 [2048], replicated
- grad_query: float32 [2048, 2048], P('dp', 'tensor')
- grad_keyval: float32 [2, 2048, 512], P(None, 'dp', 'tensor')
- grad_output: float32 [2048, 2048], P('tensor', 'dp')
- grad_gateup: float32 [2, 2048, 8192], P(None, 'dp', 'tensor')
- grad_down: float32 [8192, 2048], P('tensor', 'dp')
- change_attn_gain: float32 [2048], replicated
- change_mlp_gain: float32 [2048], replicated
- change_query: float32 [2048, 2048], P('dp', 'tensor')
- change_keyval: float32 [2, 2048, 512], P(None, 'dp', 'tensor')
- change_output: float32 [2048, 2048], P('tensor', 'dp')
- change_gateup: float32 [2, 2048, 8192], P(None, 'dp', 'tensor')
- change_down: float32 [8192, 2048], P('tensor', 'dp')
- new_m_attn_gain: float32 [2048], replicated
- new_m_mlp_gain: float32 [2048], replicated
- new_m_query: float32 [2048, 2048], P('dp', 'tensor')
- new_m_keyval: float32 [2, 2048, 512], P(None, 'dp', 'tensor')
- new_m_output: float32 [2048, 2048], P('tensor', 'dp')
- new_m_gateup: float32 [2, 2048, 8192], P(None, 'dp', 'tensor')
- new_m_down: float32 [8192, 2048], P('tensor', 'dp')
- new_s_attn_gain: float32 [2048], replicated
- new_s_mlp_gain: float32 [2048], replicated
- new_s_query: float32 [2048, 2048], P('dp', 'tensor')
- new_s_keyval: float32 [2, 2048, 512], P(None, 'dp', 'tensor')
- new_s_output: float32 [2048, 2048], P('tensor', 'dp')
- new_s_gateup: float32 [2, 2048, 8192], P(None, 'dp', 'tensor')
- new_s_down: float32 [8192, 2048], P('tensor', 'dp')
Inputs may be any that keep to these rules, and one draw needn't show every extreme that they name: `lengths`: at least one slot holds 512 real tokens.
All inputs are finite; a program needn't handle non-finite values. No bound on the sum of `lengths` on one device may be relied on, other than what follows from the above.
Results may differ from a plain program's by a relative error of at most 0.02.
Values may be sent and summed in bfloat16 or wider, within the bound.
No kernel may reach another device: no remote copies, remote signals or barrier semaphores. Data moves between devices by JAX's collectives and lax.ppermute only.
A program may use at most 256 MiB of HBM per device.

v0:
```python
import jax
import jax.numpy as jnp
from jax import lax
from jax.sharding import PartitionSpec as P


HD = 64


norm_eps = 1e-05
rope_base = 500000.0
beta_one = 0.9
beta_two = 0.999
learn_rate = 0.003
weight_decay = 0.1
adam_eps = 1e-08
adam_step = 3.0


def rotary_tables(position, half):
    position = position.astype(jnp.float32)[:, None]
    freqs = rope_base ** (-(jnp.arange(half, dtype=jnp.float32) / half))
    angle = position * freqs[None, :]
    return (jnp.cos(angle)[:, None, :], jnp.sin(angle)[:, None, :])


def rotate(vectors, cos_table, sin_table):
    half = vectors.shape[-1] // 2
    first_half = vectors[..., :half]
    second_half = vectors[..., half:]
    return jnp.concatenate(
        [
            first_half * cos_table - second_half * sin_table,
            second_half * cos_table + first_half * sin_table,
        ],
        -1,
    )


def unrotate(grads_in, cos_table, sin_table):
    half = grads_in.shape[-1] // 2
    first_half = grads_in[..., :half]
    second_half = grads_in[..., half:]
    return jnp.concatenate(
        [
            first_half * cos_table + second_half * sin_table,
            second_half * cos_table - first_half * sin_table,
        ],
        -1,
    )


def swap_pairs(size, step):
    return [(idx, idx ^ step) for idx in range(size)]


def gather_blocks(piece):
    size = lax.axis_size("tensor")
    return [piece] + [
        lax.ppermute(piece, "tensor", swap_pairs(size, step)) for step in range(1, size)
    ]


def scatter_blocks(blocks):
    size = lax.axis_size("tensor")
    total = blocks[0].astype(jnp.float32)
    for step in range(1, size):
        total = total + lax.ppermute(blocks[step], "tensor", swap_pairs(size, step)).astype(
            jnp.float32
        )
    return total


def sum_everywhere(value):
    for axis in ("tensor", "dp"):
        size = lax.axis_size(axis)
        step = 1
        while step < size:
            value = value + lax.ppermute(value, axis, swap_pairs(size, step))
            step = step * 2
    return value


def over_sequences(func, packed):
    results = [func([leaf[idx] for leaf in packed]) for idx in range(packed[0].shape[0])]
    return [jnp.stack(leaves) for leaves in zip(*results)]


def split_rows(rows):
    size = lax.axis_size("tensor")
    piece = rows.shape[1] // size
    return [rows[:, idx * piece : (idx + 1) * piece] for idx in range(size)]


def attend(query_grp, key_rot, values, allowed, score_scale):
    scores = (
        jnp.einsum("qkgd,skd->kgqs", query_grp, key_rot, preferred_element_type=jnp.float32)
        * score_scale
    )
    masked = jnp.where(allowed, scores, -1e30)
    row_max = jnp.max(masked, -1, keepdims=True)
    log_total = row_max + jnp.log(jnp.sum(jnp.exp(masked - row_max), -1, keepdims=True))
    attn_probs = jnp.exp(jnp.where(allowed, scores - log_total, -1e30))
    probs_b = attn_probs.astype(jnp.bfloat16)
    mixed = jnp.einsum("kgqs,skd->qkgd", probs_b, values, preferred_element_type=jnp.float32)
    return (mixed.astype(jnp.bfloat16), log_total)


def attend_back(query_grp, key_rot, values, log_total, grad_mixed, allowed, score_scale):
    scores = (
        jnp.einsum("qkgd,skd->kgqs", query_grp, key_rot, preferred_element_type=jnp.float32)
        * score_scale
    )
    attn_probs = jnp.exp(jnp.where(allowed, scores - log_total, -1e30))
    probs_b = attn_probs.astype(jnp.bfloat16)
    grad_probs = jnp.einsum(
        "qkgd,skd->kgqs", grad_mixed, values, preferred_element_type=jnp.float32
    )
    row_delta = jnp.sum(attn_probs * grad_probs, -1, keepdims=True)
    grad_scores = (attn_probs * (grad_probs - row_delta)).astype(jnp.bfloat16)
    grad_values = jnp.einsum(
        "kgqs,qkgd->skd", probs_b, grad_mixed, preferred_element_type=jnp.float32
    )
    grad_query = (
        jnp.einsum("kgqs,skd->qkgd", grad_scores, key_rot, preferred_element_type=jnp.float32)
        * score_scale
    )
    grad_keys = (
        jnp.einsum("kgqs,qkgd->skd", grad_scores, query_grp, preferred_element_type=jnp.float32)
        * score_scale
    )
    return (grad_query, grad_keys, grad_values)


def adamw(weight, grad, first, second, decay):
    first_new = beta_one * first + (1.0 - beta_one) * grad
    second_new = beta_two * second + (1.0 - beta_two) * grad * grad
    corr_one = 1.0 - beta_one**adam_step
    corr_two = 1.0 - beta_two**adam_step
    update = first_new / corr_one / (jnp.sqrt(second_new / corr_two) + adam_eps)
    return (-learn_rate * (update + decay * weight), first_new, second_new)


def body(
    tokens,
    cotangent,
    lengths,
    attn_gain,
    mlp_gain,
    w_query,
    w_keyval,
    w_output,
    w_gateup,
    w_down,
    m_attn_gain,
    m_mlp_gain,
    m_query,
    m_keyval,
    m_output,
    m_gateup,
    m_down,
    s_attn_gain,
    s_mlp_gain,
    s_query,
    s_keyval,
    s_output,
    s_gateup,
    s_down,
):
    bf16 = jnp.bfloat16
    f32 = jnp.float32
    seq_here, piece_len, model_width = tokens.shape
    seq_len = piece_len * lax.axis_size("tensor")
    row_count = seq_here * seq_len
    score_scale = HD ** (-0.5)
    q_cols = w_query.shape[1]
    kv_cols = w_keyval.shape[2]
    qkv_cols = q_cols + 2 * kv_cols
    here = lax.axis_index("tensor")
    position = (
        (here ^ jnp.arange(lax.axis_size("tensor"), dtype=jnp.int32))[:, None] * piece_len
        + jnp.arange(piece_len, dtype=jnp.int32)[None, :]
    ).reshape(seq_len)
    cos_table, sin_table = rotary_tables(position, HD // 2)
    attn_shard = jnp.concatenate(
        [
            w_query.astype(bf16),
            w_keyval[0].astype(bf16),
            w_keyval[1].astype(bf16),
            w_output.astype(bf16).T,
        ],
        axis=1,
    )
    attn_full = lax.all_gather(attn_shard, "dp", axis=0, tiled=True)
    gateup_full = lax.all_gather(w_gateup.astype(bf16), "dp", axis=1, tiled=True)
    down_full = lax.all_gather(w_down.astype(bf16), "dp", axis=1, tiled=True)
    qkv_full = attn_full[:, :qkv_cols]
    output_full = attn_full[:, qkv_cols:]
    x_float = tokens.astype(f32)
    inv_one = lax.rsqrt(jnp.mean(x_float * x_float, -1, keepdims=True) + norm_eps)
    normed_one = (x_float * inv_one * attn_gain).astype(bf16)
    attn_in = jnp.concatenate(gather_blocks(normed_one), axis=1).reshape(row_count, model_width)
    live_rows = position[None, :piece_len] < lengths[:, None]
    grad_piece = jnp.where(live_rows[:, :, None], cotangent, jnp.zeros_like(cotangent))
    grad_rows = jnp.concatenate(gather_blocks(grad_piece), axis=1).reshape(row_count, model_width)
    heads_here = q_cols // HD
    kv_here = kv_cols // HD
    group_size = heads_here // kv_here
    qkv_raw = jnp.dot(attn_in, qkv_full, preferred_element_type=f32)
    query_raw = qkv_raw[:, :q_cols].reshape(seq_here, seq_len, heads_here, HD)
    key_raw = qkv_raw[:, q_cols : q_cols + kv_cols].reshape(seq_here, seq_len, kv_here, HD)
    value_raw = qkv_raw[:, q_cols + kv_cols :].reshape(seq_here, seq_len, kv_here, HD)
    query_grp = (
        rotate(query_raw, cos_table, sin_table)
        .astype(bf16)
        .reshape(seq_here, seq_len, kv_here, group_size, HD)
    )
    key_rot = rotate(key_raw, cos_table, sin_table).astype(bf16)
    values = value_raw.astype(bf16)
    causal = position[None, :] <= position[:, None]

    def forward_one(packed):
        allowed = causal & (position[None, :] < packed[3])
        return attend(packed[0], packed[1], packed[2], allowed, score_scale)

    mixed, log_totals = over_sequences(forward_one, (query_grp, key_rot, values, lengths))
    mixed_flat = mixed.reshape(row_count, heads_here * HD)
    attn_part = jnp.einsum("rh,dh->rd", mixed_flat, output_full, preferred_element_type=f32)
    attn_total = scatter_blocks(
        split_rows(attn_part.astype(bf16).reshape(seq_here, seq_len, model_width))
    )
    residual = x_float + attn_total
    inv_two = lax.rsqrt(jnp.mean(residual * residual, -1, keepdims=True) + norm_eps)
    normed_two = (residual * inv_two * mlp_gain).astype(bf16)
    mlp_in = jnp.concatenate(gather_blocks(normed_two), axis=1).reshape(row_count, model_width)
    gate_proj = jnp.dot(mlp_in, gateup_full[0], preferred_element_type=f32)
    up_proj = jnp.dot(mlp_in, gateup_full[1], preferred_element_type=f32)
    sigmoid_gate = jax.nn.sigmoid(gate_proj)
    silu_gate = gate_proj * sigmoid_gate
    hidden = (silu_gate * up_proj).astype(bf16)
    mlp_part = jnp.dot(hidden, down_full, preferred_element_type=f32)
    mlp_total = scatter_blocks(
        split_rows(mlp_part.astype(bf16).reshape(seq_here, seq_len, model_width))
    )
    block_out = (residual + mlp_total).astype(bf16)
    grad_down = jnp.einsum("rf,rd->fd", hidden, grad_rows, preferred_element_type=f32)
    down_send = grad_down.astype(bf16)
    grad_rows_late, _ = lax.optimization_barrier((grad_rows, down_send))
    down_send, _ = lax.optimization_barrier((down_send, down_full))
    grad_down_s = lax.psum_scatter(down_send, "dp", scatter_dimension=1, tiled=True)
    grad_hidden = jnp.einsum("rd,fd->rf", grad_rows_late, down_full, preferred_element_type=f32)
    grad_gate = (
        grad_hidden * up_proj * sigmoid_gate * (1.0 + gate_proj * (1.0 - sigmoid_gate))
    ).astype(bf16)
    grad_up = (grad_hidden * silu_gate).astype(bf16)
    grad_in_two = jnp.einsum(
        "rf,df->rd", grad_gate, gateup_full[0], preferred_element_type=f32
    ) + jnp.einsum("rf,df->rd", grad_up, gateup_full[1], preferred_element_type=f32)
    grad_in_two = grad_in_two.astype(bf16)
    mlp_in_late, _ = lax.optimization_barrier((mlp_in, grad_in_two))
    grad_normed_two = scatter_blocks(
        split_rows(grad_in_two.reshape(seq_here, seq_len, model_width))
    )
    gate_send = jnp.einsum(
        "rd,rf->df", mlp_in_late, grad_gate, preferred_element_type=f32
    ).astype(bf16)
    up_send = jnp.einsum("rd,rf->df", mlp_in_late, grad_up, preferred_element_type=f32).astype(bf16)
    grad_gate_s = lax.psum_scatter(gate_send, "dp", scatter_dimension=0, tiled=True)
    grad_up_s = lax.psum_scatter(up_send, "dp", scatter_dimension=0, tiled=True)
    grad_normed_two, _, _ = lax.optimization_barrier((grad_normed_two, gate_send, up_send))
    scaled_two = mlp_gain * grad_normed_two
    gain_two_part = jnp.sum(grad_normed_two * residual * inv_two, axis=(0, 1))
    grad_resid = (
        grad_piece.astype(f32)
        + inv_two * scaled_two
        - residual * inv_two**3 * jnp.mean(scaled_two * residual, -1, keepdims=True)
    )
    grad_resid_b = grad_resid.astype(bf16)
    grad_attn_rows = jnp.concatenate(gather_blocks(grad_resid_b), axis=1).reshape(
        row_count, model_width
    )
    grad_attn_rows, _ = lax.optimization_barrier((grad_attn_rows, grad_down_s))
    grad_out_w = jnp.einsum("rd,rh->dh", grad_attn_rows, mixed_flat, preferred_element_type=f32)
    grad_mixed = jnp.dot(grad_attn_rows, output_full, preferred_element_type=f32).astype(bf16)
    grad_mixed = grad_mixed.reshape(seq_here, seq_len, kv_here, group_size, HD)

    def backward_one(packed):
        allowed = causal & (position[None, :] < packed[5])
        return attend_back(
            packed[0], packed[1], packed[2], packed[3], packed[4], allowed, score_scale
        )

    grad_q, grad_k, grad_v = over_sequences(
        backward_one, (query_grp, key_rot, values, log_totals, grad_mixed, lengths)
    )
    grad_q_b = unrotate(
        grad_q.reshape(seq_here, seq_len, heads_here, HD), cos_table, sin_table
    ).astype(bf16)
    grad_q_b = grad_q_b.reshape(row_count, heads_here * HD)
    grad_k_b = unrotate(grad_k, cos_table, sin_table).astype(bf16).reshape(row_count, kv_here * HD)
    grad_v_b = grad_v.astype(bf16).reshape(row_count, kv_here * HD)
    grad_qkv_b = jnp.concatenate([grad_q_b, grad_k_b, grad_v_b], axis=1)
    grad_qkv_w = jnp.einsum("rd,rh->dh", attn_in, grad_qkv_b, preferred_element_type=f32)
    grad_in_one = jnp.einsum("rh,dh->rd", grad_qkv_b, qkv_full, preferred_element_type=f32)
    grad_normed_one = scatter_blocks(
        split_rows(grad_in_one.astype(bf16).reshape(seq_here, seq_len, model_width))
    )
    scaled_one = attn_gain * grad_normed_one
    gain_one_part = jnp.sum(grad_normed_one * x_float * inv_one, axis=(0, 1))
    input_grad = (
        grad_resid
        + inv_one * scaled_one
        - x_float * inv_one**3 * jnp.mean(scaled_one * x_float, -1, keepdims=True)
    )
    gain_grads = sum_everywhere(jnp.stack([gain_one_part, gain_two_part]))
    attn_send = jnp.concatenate([grad_qkv_w.astype(bf16), grad_out_w.astype(bf16)], axis=1)
    grad_attn_s = lax.psum_scatter(attn_send, "dp", scatter_dimension=0, tiled=True).astype(f32)
    grad_down_s = grad_down_s.astype(f32)
    grad_gate_s = grad_gate_s.astype(f32)
    grad_up_s = grad_up_s.astype(f32)
    grads_all = (
        gain_grads[0],
        gain_grads[1],
        grad_attn_s[:, :q_cols],
        jnp.stack(
            [grad_attn_s[:, q_cols : q_cols + kv_cols], grad_attn_s[:, q_cols + kv_cols : qkv_cols]]
        ),
        grad_attn_s[:, qkv_cols:].T,
        jnp.stack([grad_gate_s, grad_up_s]),
        grad_down_s,
    )
    params = (attn_gain, mlp_gain, w_query, w_keyval, w_output, w_gateup, w_down)
    firsts = (m_attn_gain, m_mlp_gain, m_query, m_keyval, m_output, m_gateup, m_down)
    seconds = (s_attn_gain, s_mlp_gain, s_query, s_keyval, s_output, s_gateup, s_down)
    decays = (0.0, 0.0, weight_decay, weight_decay, weight_decay, weight_decay, weight_decay)
    updated = [
        adamw(params[idx], grads_all[idx], firsts[idx], seconds[idx], decays[idx])
        for idx in range(7)
    ]
    return (
        block_out,
        input_grad,
        grads_all[0],
        grads_all[1],
        grads_all[2],
        grads_all[3],
        grads_all[4],
        grads_all[5],
        grads_all[6],
        updated[0][0],
        updated[1][0],
        updated[2][0],
        updated[3][0],
        updated[4][0],
        updated[5][0],
        updated[6][0],
        updated[0][1],
        updated[1][1],
        updated[2][1],
        updated[3][1],
        updated[4][1],
        updated[5][1],
        updated[6][1],
        updated[0][2],
        updated[1][2],
        updated[2][2],
        updated[3][2],
        updated[4][2],
        updated[5][2],
        updated[6][2],
    )


def solution(mesh):
    placed = (
        P("dp", "tensor", None),
        P("dp", "tensor", None),
        P("dp"),
        P(),
        P(),
        P("dp", "tensor"),
        P(None, "dp", "tensor"),
        P("tensor", "dp"),
        P(None, "dp", "tensor"),
        P("tensor", "dp"),
        P(),
        P(),
        P("dp", "tensor"),
        P(None, "dp", "tensor"),
        P("tensor", "dp"),
        P(None, "dp", "tensor"),
        P("tensor", "dp"),
        P(),
        P(),
        P("dp", "tensor"),
        P(None, "dp", "tensor"),
        P("tensor", "dp"),
        P(None, "dp", "tensor"),
        P("tensor", "dp"),
    )

    return jax.shard_map(
        body,
        mesh=mesh,
        in_specs=placed,
        out_specs=(
            P("dp", "tensor", None),
            P("dp", "tensor", None),
            P(),
            P(),
            P("dp", "tensor"),
            P(None, "dp", "tensor"),
            P("tensor", "dp"),
            P(None, "dp", "tensor"),
            P("tensor", "dp"),
            P(),
            P(),
            P("dp", "tensor"),
            P(None, "dp", "tensor"),
            P("tensor", "dp"),
            P(None, "dp", "tensor"),
            P("tensor", "dp"),
            P(),
            P(),
            P("dp", "tensor"),
            P(None, "dp", "tensor"),
            P("tensor", "dp"),
            P(None, "dp", "tensor"),
            P("tensor", "dp"),
            P(),
            P(),
            P("dp", "tensor"),
            P(None, "dp", "tensor"),
            P("tensor", "dp"),
            P(None, "dp", "tensor"),
            P("tensor", "dp"),
        ),
        check_vma=False,
    )
```

profile of v0, /device:TPU:0, one launch (start us, length us, event | category | flops | bytes accessed | tf_op | source)
XLA Modules:
  0.0 708.3 jit_solution(7300385531575127179)
XLA Ops:
  27.1 18.9 %collective-permute-done = bf16[2,128,2048]{2,1,0:T(8,128)(2,1)} collective-permute-done((bf16[2,128,2048]{2,1,0:T(8,128)(2,1)}, bf16[2,128,2048]{2,1,0:T(8,128)(2,1)}, u32[]{:S(2)}, u32[]{:S(2)}) %collective-permute-start) | collective-permute-done | bytes 1048608 | tf_op jit(solution)/shard_map/ppermute | solution.py:60
  46.0 23.1 %collective-permute-done.1 = bf16[2,128,2048]{2,1,0:T(8,128)(2,1)} collective-permute-done((bf16[2,128,2048]{2,1,0:T(8,128)(2,1)}, bf16[2,128,2048]{2,1,0:T(8,128)(2,1)}, u32[]{:S(2)}, u32[]{:S(2)}) %collective-permute-start.1) | collective-permute-done | bytes 1048608 | tf_op jit(solution)/shard_map/ppermute | solution.py:60
  119.7 19.6 %collective-permute-done.3 = bf16[2,128,2048]{2,1,0:T(8,128)(2,1)S(1)} collective-permute-done((bf16[2,128,2048]{2,1,0:T(8,128)(2,1)S(1)}, bf16[2,128,2048]{2,1,0:T(8,128)(2,1)S(1)}, u32[]{:S(2)}, u32[]{:S(2)}) %collective-permute-start.3) | collective-permute-done | bytes 1048608 | tf_op jit(solution)/shard_map/ppermute | solution.py:68
  140.9 22.2 %collective-permute-done.4 = bf16[2,128,2048]{2,1,0:T(8,128)(2,1)S(1)} collective-permute-done((bf16[2,128,2048]{2,1,0:T(8,128)(2,1)S(1)}, bf16[2,128,2048]{2,1,0:T(8,128)(2,1)S(1)}, u32[]{:S(2)}, u32[]{:S(2)}) %collective-permute-start.4) | collective-permute-done | bytes 1048608 | tf_op jit(solution)/shard_map/ppermute | solution.py:68
  167.9 16.4 %collective-permute-done.12 = bf16[2,128,2048]{2,1,0:T(8,128)(2,1)S(1)} collective-permute-done((bf16[2,128,2048]{2,1,0:T(8,128)(2,1)S(1)}, bf16[2,128,2048]{2,1,0:T(8,128)(2,1)S(1)}, u32[]{:S(2)}, u32[]{:S(2)}) %collective-permute-start.12) | collective-permute-done | bytes 1048608 | tf_op jit(solution)/shard_map/ppermute | solution.py:60
  185.9 22.2 %collective-permute-done.13 = bf16[2,128,2048]{2,1,0:T(8,128)(2,1)S(1)} collective-permute-done((bf16[2,128,2048]{2,1,0:T(8,128)(2,1)S(1)}, bf16[2,128,2048]{2,1,0:T(8,128)(2,1)S(1)}, u32[]{:S(2)}, u32[]{:S(2)}) %collective-permute-start.13) | collective-permute-done | bytes 1048608 | tf_op jit(solution)/shard_map/ppermute | solution.py:60
  210.3 18.9 %collective-permute-done.6 = bf16[2,128,2048]{2,1,0:T(8,128)(2,1)S(1)} collective-permute-done((bf16[2,128,2048]{2,1,0:T(8,128)(2,1)S(1)}, bf16[2,128,2048]{2,1,0:T(8,128)(2,1)S(1)}, u32[]{:S(2)}, u32[]{:S(2)}) %collective-permute-start.6) | collective-permute-done | bytes 1048608 | tf_op jit(solution)/shard_map/ppermute | solution.py:60
  229.3 22.0 %collective-permute-done.7 = bf16[2,128,2048]{2,1,0:T(8,128)(2,1)S(1)} collective-permute-done((bf16[2,128,2048]{2,1,0:T(8,128)(2,1)S(1)}, bf16[2,128,2048]{2,1,0:T(8,128)(2,1)S(1)}, u32[]{:S(2)}, u32[]{:S(2)}) %collective-permute-start.7) | collective-permute-done | bytes 1048608 | tf_op jit(solution)/shard_map/ppermute | solution.py:60
  253.5 13.5 %fusion.14 = f32[1024,2048]{1,0:T(8,128)S(1)} fusion(bf16[1024,2048]{1,0:T(8,128)(2,1)} %bitcast.284, bf16[2,2048,2048]{2,1,0:T(8,128)(2,1)} %all-gather.6.cloned.1.call-done), kind=kOutput, calls=%fused_computation.34 | convolution fusion | flops 8589934592 | bytes 20971520 | tf_op jit(solution)/shard_map/dot_general | solution.py:236
  267.0 18.0 %multiply_convert_fusion.2 = (bf16[1024,2048]{1,0:T(8,128)(2,1)}, f32[1024,2048]{1,0:T(8,128)}) fusion(f32[1024,2048]{1,0:T(8,128)S(1)} %fusion.14, bf16[1024,2048]{1,0:T(8,128)(2,1)S(1)} %bitcast.286, bf16[2,2048,2048]{2,1,0:T(8,128)(2,1)} %all-gather.6.cloned.1.call-done), kind=kOutput, calls=%fused_computation.23 | convolution fusion | flops 8602517504 | bytes 33554432 | tf_op jit(solution)/shard_map/dot_general | solution.py:237
  285.1 13.5 %convolution_convert_fusion.2 = bf16[2048,2048]{1,0:T(8,128)(2,1)} fusion(bf16[1024,2048]{1,0:T(8,128)(2,1)} %get-tuple-element.222, bf16[1024,2048]{1,0:T(8,128)(2,1)S(1)} %bitcast.291), kind=kOutput, calls=%fused_computation.32 | convolution fusion | flops 8594128896 | bytes 16777216 | tf_op jit(solution)/shard_map/rf,rd->fd/dot_general | solution.py:246
  306.3 20.8 %multiply_convert_fusion = (bf16[1024,2048]{1,0:T(8,128)(2,1)S(1)}, bf16[1024,2048]{1,0:T(8,128)(2,1)}) fusion(f32[1024,2048]{1,0:T(8,128)} %copy-done.80, f32[1024,2048]{1,0:T(8,128)} %get-tuple-element.223, bf16[1024,2048]{1,0:T(8,128)(2,1)} %bitcast.290, bf16[2048,2048]{1,0:T(8,128)(2,1)} %all-gather.8.cloned.1.call-done), kind=kOutput, calls=%fused_computation.21 | convolution fusion | flops 8617197568 | bytes 37748736 | tf_op jit(solution)/shard_map/rd,fd->rf/dot_general | solution.py:251
  327.0 12.6 %fusion.13 = f32[1024,2048]{1,0:T(8,128)S(1)} fusion(bf16[1024,2048]{1,0:T(8,128)(2,1)} %get-tuple-element.161, bf16[2,2048,2048]{2,1,0:T(8,128)(2,1)} %all-gather.6.cloned.1.call-done), kind=kOutput, calls=%fused_computation.33 | convolution fusion | flops 8589934592 | bytes 20971520 | tf_op jit(solution)/shard_map/rf,df->rd/dot_general | solution.py:256
  339.7 13.6 %add_convert_fusion = bf16[1024,2048]{1,0:T(8,128)(2,1)} fusion(f32[1024,2048]{1,0:T(8,128)S(1)} %fusion.13, bf16[1024,2048]{1,0:T(8,128)(2,1)S(1)} %get-tuple-element.160, bf16[2,2048,2048]{2,1,0:T(8,128)(2,1)} %all-gather.6.cloned.1.call-done), kind=kOutput, calls=%fused_computation.20 | convolution fusion | flops 8594128896 | bytes 25165824 | tf_op jit(solution)/shard_map/rf,df->rd/dot_general | solution.py:258
  353.3 11.4 %convolution_convert_fusion = bf16[2048,2048]{1,0:T(8,128)(2,1)} fusion(bf16[1024,2048]{1,0:T(8,128)(2,1)S(1)} %bitcast.287, bf16[1024,2048]{1,0:T(8,128)(2,1)S(1)} %get-tuple-element.160), kind=kOutput, calls=%fused_computation.30 | convolution fusion | flops 8594128896 | bytes 16777216 | tf_op jit(solution)/shard_map/rd,rf->df/dot_general | solution.py:267
  364.7 14.3 %convolution_convert_fusion.1 = bf16[2048,2048]{1,0:T(8,128)(2,1)} fusion(bf16[1024,2048]{1,0:T(8,128)(2,1)} %bitcast.285, bf16[1024,2048]{1,0:T(8,128)(2,1)} %get-tuple-element.161), kind=kOutput, calls=%fused_computation.31 | convolution fusion | flops 8594128896 | bytes 16777216 | tf_op jit(solution)/shard_map/rd,rf->df/dot_general | solution.py:264
  408.9 44.9 %collective-permute-done.16 = bf16[2,128,2048]{2,1,0:T(8,128)(2,1)S(1)} collective-permute-done((bf16[2,128,2048]{2,1,0:T(8,128)(2,1)S(1)}, bf16[2,128,2048]{2,1,0:T(8,128)(2,1)S(1)}, u32[]{:S(2)}, u32[]{:S(2)}) %collective-permute-start.16) | collective-permute-done | bytes 1048608 | tf_op jit(solution)/shard_map/ppermute | solution.py:68
  456.4 19.1 %collective-permute-done.10 = bf16[2,128,2048]{2,1,0:T(8,128)(2,1)S(1)} collective-permute-done((bf16[2,128,2048]{2,1,0:T(8,128)(2,1)S(1)}, bf16[2,128,2048]{2,1,0:T(8,128)(2,1)S(1)}, u32[]{:S(2)}, u32[]{:S(2)}) %collective-permute-start.10) | collective-permute-done | bytes 1048608 | tf_op jit(solution)/shard_map/ppermute | solution.py:68
  481.3 22.5 %collective-permute-done.18 = bf16[2,128,2048]{2,1,0:T(8,128)(2,1)S(1)} collective-permute-done((bf16[2,128,2048]{2,1,0:T(8,128)(2,1)S(1)}, bf16[2,128,2048]{2,1,0:T(8,128)(2,1)S(1)}, u32[]{:S(2)}, u32[]{:S(2)}) %collective-permute-start.18) | collective-permute-done | bytes 1048608 | tf_op jit(solution)/shard_map/ppermute | solution.py:60
  503.8 21.8 %collective-permute-done.20 = bf16[2,128,2048]{2,1,0:T(8,128)(2,1)S(1)} collective-permute-done((bf16[2,128,2048]{2,1,0:T(8,128)(2,1)S(1)}, bf16[2,128,2048]{2,1,0:T(8,128)(2,1)S(1)}, u32[]{:S(2)}, u32[]{:S(2)}) %collective-permute-start.20) | collective-permute-done | bytes 1048608 | tf_op jit(solution)/shard_map/ppermute | solution.py:60
  555.3 15.8 %fusion.2 = (bf16[2,4,512,512]{2,3,1,0:T(8,128)(2,1)S(1)}, bf16[2,4,512,512]{2,3,1,0:T(8,128)(2,1)}) fusion(f32[2,512,512,4]{2,1,3,0:T(8,128)} %get-tuple-element.225, f32[2,512,512,4]{2,1,3,0:T(8,128)} %copy-done.1, f32[2,4,512]{2,1,0:T(4,128)S(1)} %get-tuple-element.224, f32[2,4,512]{2,1,0:T(4,128)S(1)} %bitcast.322, pred[512,512]{0,1:T(8,128)(4,1)S(1)} %copy-done.12, ...), kind=kLoop, calls=%fused_computation.6 | loop fusion | flops 25165824 | bytes 42532864 | tf_op jit(solution)/shard_map/convert_element_type | solution.py:120
  600.8 22.5 %collective-permute-done.21 = bf16[2,128,2048]{2,1,0:T(8,128)(2,1)S(1)} collective-permute-done((bf16[2,128,2048]{2,1,0:T(8,128)(2,1)S(1)}, bf16[2,128,2048]{2,1,0:T(8,128)(2,1)S(1)}, u32[]{:S(2)}, u32[]{:S(2)}) %collective-permute-start.21) | collective-permute-done | bytes 1048608 | tf_op jit(solution)/shard_map/ppermute | solution.py:68
  623.4 20.6 %collective-permute-done.22 = bf16[2,128,2048]{2,1,0:T(8,128)(2,1)S(1)} collective-permute-done((bf16[2,128,2048]{2,1,0:T(8,128)(2,1)S(1)}, bf16[2,128,2048]{2,1,0:T(8,128)(2,1)S(1)}, u32[]{:S(2)}, u32[]{:S(2)}) %collective-permute-start.22) | collective-permute-done | bytes 1048608 | tf_op jit(solution)/shard_map/ppermute | solution.py:68
  654.8 11.9 %add_multiply_fusion = (f32[2,256,2048]{2,1,0:T(8,128)}, f32[2,256,2048]{2,1,0:T(8,128)}, f32[2,256,2048]{2,1,0:T(8,128)}, f32[2,256,2048]{2,1,0:T(8,128)}) fusion(f32[2,256,2048]{2,1,0:T(8,128)} %param.32, f32[2,256,2048]{2,1,0:T(8,128)} %param.39, f32[2,256,2048]{2,1,0:T(8,128)} %param.46, bf16[1,256,2048]{2,1,0:T(8,128)(2,1)} %bitcast.301, ...), kind=kLoop, calls=%fused_computation.52 | loop fusion | flops 16777216 | bytes 31457280 | tf_op jit(solution)/shard_map/mul | solution.py:141
  (359 shorter events, 232.3 us)
Async XLA Ops:
  7.2 65.7 %all-gather.4.cloned.1.call-start = ((), (), s32[]{:S(2)}) async-start(), calls=%async_computation.4 | async-start | bytes 5898240 | tf_op jit(solution)/shard_map/all_gather | solution.py:194
  12.5 241.0 %all-gather.6.cloned.1.call-start = ((), (), s32[]{:S(2)}) async-start(), calls=%async_computation.5 | async-start | bytes 18874368 | tf_op jit(solution)/shard_map/all_gather | solution.py:195
  16.5 289.7 %all-gather.8.cloned.1.call-start = ((), (), s32[]{:S(2)}) async-start(), calls=%async_computation.6 | async-start | bytes 9437184 | tf_op jit(solution)/shard_map/all_gather | solution.py:196
  21.7 47.4 %collective-permute-start.1 = (bf16[2,128,2048]{2,1,0:T(8,128)(2,1)}, bf16[2,128,2048]{2,1,0:T(8,128)(2,1)}, u32[]{:S(2)}, u32[]{:S(2)}) collective-permute-start(bf16[2,128,2048]{2,1,0:T(8,128)(2,1)} %fusion.26), channel_id=1, source_target_pairs={{0,2},{1,3},{2,0},{3,1},{4,6},{5,7},{6,4},{7,5},{8,10},{9,11},{10,... | collective-permute-start | bytes 3145736 | tf_op jit(solution)/shard_map/ppermute | solution.py:60
  23.2 45.9 %collective-permute-start.2 = (bf16[2,128,2048]{2,1,0:T(8,128)(2,1)}, bf16[2,128,2048]{2,1,0:T(8,128)(2,1)}, u32[]{:S(2)}, u32[]{:S(2)}) collective-permute-start(bf16[2,128,2048]{2,1,0:T(8,128)(2,1)} %fusion.26), channel_id=1, source_target_pairs={{0,3},{1,2},{2,1},{3,0},{4,7},{5,6},{6,5},{7,4},{8,11},{9,10},{10,... | collective-permute-start | bytes 3145736 | tf_op jit(solution)/shard_map/ppermute | solution.py:60
  24.3 503.8 %reduce-scatter.5.cloned.1.call-start = ((), (), s32[]{:S(2)}) async-start(), calls=%async_computation.7 | async-start | bytes 9437184 | tf_op jit(solution)/shard_map/reduce_scatter | solution.py:250
  114.6 48.5 %collective-permute-start.4 = (bf16[2,128,2048]{2,1,0:T(8,128)(2,1)S(1)}, bf16[2,128,2048]{2,1,0:T(8,128)(2,1)S(1)}, u32[]{:S(2)}, u32[]{:S(2)}) collective-permute-start(bf16[2,128,2048]{2,1,0:T(8,128)(2,1)S(1)} %get-tuple-element.173), channel_id=1, source_target_pairs={{0,2},{1,3},{2,0},{3,1},{4,6},{5,7},{6,4},{7,5},{8,10},{9,11},{10,... | collective-permute-start | bytes 3145736 | tf_op jit(solution)/shard_map/ppermute | solution.py:68
  115.4 47.7 %collective-permute-start.5 = (bf16[2,128,2048]{2,1,0:T(8,128)(2,1)S(1)}, bf16[2,128,2048]{2,1,0:T(8,128)(2,1)S(1)}, u32[]{:S(2)}, u32[]{:S(2)}) collective-permute-start(bf16[2,128,2048]{2,1,0:T(8,128)(2,1)S(1)} %get-tuple-element.172), channel_id=1, source_target_pairs={{0,3},{1,2},{2,1},{3,0},{4,7},{5,6},{6,5},{7,4},{8,11},{9,10},{10,... | collective-permute-start | bytes 3145736 | tf_op jit(solution)/shard_map/ppermute | solution.py:68
  117.5 66.8 %collective-permute-start.12 = (bf16[2,128,2048]{2,1,0:T(8,128)(2,1)S(1)}, bf16[2,128,2048]{2,1,0:T(8,128)(2,1)S(1)}, u32[]{:S(2)}, u32[]{:S(2)}) collective-permute-start(bf16[2,128,2048]{2,1,0:T(8,128)(2,1)S(1)} %broadcast_select_fusion), channel_id=1, source_target_pairs={{0,1},{1,0},{2,3},{3,2},{4,5},{5,4},{6,7},{7,6},{8,9},{9,8},{10,11... | collective-permute-start | bytes 3145736 | tf_op jit(solution)/shard_map/ppermute | solution.py:60
  118.9 89.1 %collective-permute-start.13 = (bf16[2,128,2048]{2,1,0:T(8,128)(2,1)S(1)}, bf16[2,128,2048]{2,1,0:T(8,128)(2,1)S(1)}, u32[]{:S(2)}, u32[]{:S(2)}) collective-permute-start(bf16[2,128,2048]{2,1,0:T(8,128)(2,1)S(1)} %broadcast_select_fusion), channel_id=1, source_target_pairs={{0,2},{1,3},{2,0},{3,1},{4,6},{5,7},{6,4},{7,5},{8,10},{9,11},{10,... | collective-permute-start | bytes 3145736 | tf_op jit(solution)/shard_map/ppermute | solution.py:60
  139.3 68.8 %collective-permute-start.14 = (bf16[2,128,2048]{2,1,0:T(8,128)(2,1)S(1)}, bf16[2,128,2048]{2,1,0:T(8,128)(2,1)S(1)}, u32[]{:S(2)}, u32[]{:S(2)}) collective-permute-start(bf16[2,128,2048]{2,1,0:T(8,128)(2,1)S(1)} %broadcast_select_fusion), channel_id=1, source_target_pairs={{0,3},{1,2},{2,1},{3,0},{4,7},{5,6},{6,5},{7,4},{8,11},{9,10},{10,... | collective-permute-start | bytes 3145736 | tf_op jit(solution)/shard_map/ppermute | solution.py:60
  165.6 63.7 %collective-permute-start.6 = (bf16[2,128,2048]{2,1,0:T(8,128)(2,1)S(1)}, bf16[2,128,2048]{2,1,0:T(8,128)(2,1)S(1)}, u32[]{:S(2)}, u32[]{:S(2)}) collective-permute-start(bf16[2,128,2048]{2,1,0:T(8,128)(2,1)S(1)} %multiply_convert_fusion.3), channel_id=1, source_target_pairs={{0,1},{1,0},{2,3},{3,2},{4,5},{5,4},{6,7},{7,6},{8,9},{9,8},{10,11... | collective-permute-start | bytes 3145736 | tf_op jit(solution)/shard_map/ppermute | solution.py:60
  166.3 84.9 %collective-permute-start.7 = (bf16[2,128,2048]{2,1,0:T(8,128)(2,1)S(1)}, bf16[2,128,2048]{2,1,0:T(8,128)(2,1)S(1)}, u32[]{:S(2)}, u32[]{:S(2)}) collective-permute-start(bf16[2,128,2048]{2,1,0:T(8,128)(2,1)S(1)} %multiply_convert_fusion.3), channel_id=1, source_target_pairs={{0,2},{1,3},{2,0},{3,1},{4,6},{5,7},{6,4},{7,5},{8,10},{9,11},{10,... | collective-permute-start | bytes 3145736 | tf_op jit(solution)/shard_map/ppermute | solution.py:60
  184.3 66.9 %collective-permute-start.8 = (bf16[2,128,2048]{2,1,0:T(8,128)(2,1)S(1)}, bf16[2,128,2048]{2,1,0:T(8,128)(2,1)S(1)}, u32[]{:S(2)}, u32[]{:S(2)}) collective-permute-start(bf16[2,128,2048]{2,1,0:T(8,128)(2,1)S(1)} %multiply_convert_fusion.3), channel_id=1, source_target_pairs={{0,3},{1,2},{2,1},{3,0},{4,7},{5,6},{6,5},{7,4},{8,11},{9,10},{10,... | collective-permute-start | bytes 3145736 | tf_op jit(solution)/shard_map/ppermute | solution.py:60
  306.2 348.6 %reduce-scatter.11.cloned.1.call-start = ((), (), s32[]{:S(2)}) async-start(), calls=%async_computation.10 | async-start | bytes 9437184 | tf_op jit(solution)/shard_map/reduce_scatter | solution.py:269
  364.7 290.1 %reduce-scatter.9.cloned.1.call-start = ((), (), s32[]{:S(2)}) async-start(), calls=%async_computation.9 | async-start | bytes 9437184 | tf_op jit(solution)/shard_map/reduce_scatter | solution.py:268
  379.0 302.7 %reduce-scatter.7.cloned.1.call-start = ((), (), s32[]{:S(2)}) async-start(), calls=%async_computation.8 | async-start | bytes 5898240 | tf_op jit(solution)/shard_map/reduce_scatter | solution.py:317
  382.8 71.0 %collective-permute-start.16 = (bf16[2,128,2048]{2,1,0:T(8,128)(2,1)S(1)}, bf16[2,128,2048]{2,1,0:T(8,128)(2,1)S(1)}, u32[]{:S(2)}, u32[]{:S(2)}) collective-permute-start(bf16[2,128,2048]{2,1,0:T(8,128)(2,1)S(1)} %get-tuple-element.167), channel_id=1, source_target_pairs={{0,2},{1,3},{2,0},{3,1},{4,6},{5,7},{6,4},{7,5},{8,10},{9,11},{10,... | collective-permute-start | bytes 3145736 | tf_op jit(solution)/shard_map/ppermute | solution.py:68
  384.3 69.5 %collective-permute-start.17 = (bf16[2,128,2048]{2,1,0:T(8,128)(2,1)S(1)}, bf16[2,128,2048]{2,1,0:T(8,128)(2,1)S(1)}, u32[]{:S(2)}, u32[]{:S(2)}) collective-permute-start(bf16[2,128,2048]{2,1,0:T(8,128)(2,1)S(1)} %get-tuple-element.166), channel_id=1, source_target_pairs={{0,3},{1,2},{2,1},{3,0},{4,7},{5,6},{6,5},{7,4},{8,11},{9,10},{10,... | collective-permute-start | bytes 3145736 | tf_op jit(solution)/shard_map/ppermute | solution.py:68
  396.6 78.9 %collective-permute-start.10 = (bf16[2,128,2048]{2,1,0:T(8,128)(2,1)S(1)}, bf16[2,128,2048]{2,1,0:T(8,128)(2,1)S(1)}, u32[]{:S(2)}, u32[]{:S(2)}) collective-permute-start(bf16[2,128,2048]{2,1,0:T(8,128)(2,1)S(1)} %get-tuple-element.170), channel_id=1, source_target_pairs={{0,2},{1,3},{2,0},{3,1},{4,6},{5,7},{6,4},{7,5},{8,10},{9,11},{10,... | collective-permute-start | bytes 3145736 | tf_op jit(solution)/shard_map/ppermute | solution.py:68
  398.1 77.4 %collective-permute-start.11 = (bf16[2,128,2048]{2,1,0:T(8,128)(2,1)S(1)}, bf16[2,128,2048]{2,1,0:T(8,128)(2,1)S(1)}, u32[]{:S(2)}, u32[]{:S(2)}) collective-permute-start(bf16[2,128,2048]{2,1,0:T(8,128)(2,1)S(1)} %get-tuple-element.169), channel_id=1, source_target_pairs={{0,3},{1,2},{2,1},{3,0},{4,7},{5,6},{6,5},{7,4},{8,11},{9,10},{10,... | collective-permute-start | bytes 3145736 | tf_op jit(solution)/shard_map/ppermute | solution.py:68
  407.5 68.0 %collective-permute-start.9 = (bf16[2,128,2048]{2,1,0:T(8,128)(2,1)S(1)}, bf16[2,128,2048]{2,1,0:T(8,128)(2,1)S(1)}, u32[]{:S(2)}, u32[]{:S(2)}) collective-permute-start(bf16[2,128,2048]{2,1,0:T(8,128)(2,1)S(1)} %get-tuple-element.168), channel_id=1, source_target_pairs={{0,1},{1,0},{2,3},{3,2},{4,5},{5,4},{6,7},{7,6},{8,9},{9,8},{10,11... | collective-permute-start | bytes 3145736 | tf_op jit(solution)/shard_map/ppermute | solution.py:68
  479.8 45.8 %collective-permute-start.20 = (bf16[2,128,2048]{2,1,0:T(8,128)(2,1)S(1)}, bf16[2,128,2048]{2,1,0:T(8,128)(2,1)S(1)}, u32[]{:S(2)}, u32[]{:S(2)}) collective-permute-start(bf16[2,128,2048]{2,1,0:T(8,128)(2,1)S(1)} %get-tuple-element.178), channel_id=1, source_target_pairs={{0,3},{1,2},{2,1},{3,0},{4,7},{5,6},{6,5},{7,4},{8,11},{9,10},{10,... | collective-permute-start | bytes 3145736 | tf_op jit(solution)/shard_map/ppermute | solution.py:60
  598.3 45.7 %collective-permute-start.22 = (bf16[2,128,2048]{2,1,0:T(8,128)(2,1)S(1)}, bf16[2,128,2048]{2,1,0:T(8,128)(2,1)S(1)}, u32[]{:S(2)}, u32[]{:S(2)}) collective-permute-start(bf16[2,128,2048]{2,1,0:T(8,128)(2,1)S(1)} %get-tuple-element.164), channel_id=1, source_target_pairs={{0,2},{1,3},{2,0},{3,1},{4,6},{5,7},{6,4},{7,5},{8,10},{9,11},{10,... | collective-permute-start | bytes 3145736 | tf_op jit(solution)/shard_map/ppermute | solution.py:68
  (98 other events, 1662.7 us)
Sparse Core Ops, SparseCore 0:
  12.6 59.1 all-gather.3
  74.0 149.2 all-gather.5
  225.5 80.6 all-gather.7
  308.3 87.6 reduce-scatter.4
  398.2 87.9 reduce-scatter.10
  488.4 87.9 reduce-scatter.8
  591.3 57.4 reduce-scatter.6
where the time goes:
time: 714 us; the launch traced here: 708 us
  waiting for transfers between devices  334 us (47%)
  matrix products  194 us (27%)
  other arithmetic  85.2 us (12%)
  local copies, waits for them, and re-layouts  44.8 us (6%)
  starting transfers between devices  34.2 us (5%)
  between operations  16 us (2%)
    ppermute x12, waiting for transfers between devices, gather_blocks(): lax.ppermute(piece, 'tensor', swap_pairs(size, step))  166 us
    ppermute x12, waiting for transfers between devices, scatter_blocks(): lax.ppermute(blocks[step], 'tensor', swap_pairs(size, step))  157 us
    mul x7, other arithmetic, adamw(): return (-learn_rate * (update + decay * weight), first_new, second_new)  24.9 us
    unnamed x192, local copies, waits for them, and re-layouts  24.4 us
    dot_general x1, matrix products, body(): jnp.einsum('rd,fd->rf', grad_rows_late, down_full, preferred_element_type...  20.8 us
    dot_general x1, matrix products, body(): up_proj = jnp.dot(mlp_in, gateup_full[1], preferred_element_type=f32)  18 us
    convert_element_type x1, other arithmetic, attend_back(): grad_scores = (attn_probs * (grad_probs - row_delta)).astype(jnp.bfloat16)  15.8 us
    ppermute x12, starting transfers between devices, gather_blocks(): lax.ppermute(piece, 'tensor', swap_pairs(size, step))  15.7 us
  transfers between devices with their start and end apart: 36, of which 17 were waited for; matrix products, arithmetic and copies ran while one was open for 42% of the time, Pallas kernels for 0%

commit v1 on v0

--- a/solution.py
+++ b/solution.py
@@ -242,7 +242,6 @@
     mlp_total = scatter_blocks(
         split_rows(mlp_part.astype(bf16).reshape(seq_here, seq_len, model_width))
     )
-    block_out = (residual + mlp_total).astype(bf16)
     grad_down = jnp.einsum("rf,rd->fd", hidden, grad_rows, preferred_element_type=f32)
     down_send = grad_down.astype(bf16)
     grad_rows_late, _ = lax.optimization_barrier((grad_rows, down_send))
@@ -279,7 +278,10 @@
     grad_attn_rows = jnp.concatenate(gather_blocks(grad_resid_b), axis=1).reshape(
         row_count, model_width
     )
-    grad_attn_rows, _ = lax.optimization_barrier((grad_attn_rows, grad_down_s))
+    new_down = adamw(w_down, grad_down_s.astype(f32), m_down, s_down, weight_decay)
+    residual_late, _ = lax.optimization_barrier((residual, grad_attn_rows))
+    block_out = (residual_late + mlp_total).astype(bf16)
+    grad_attn_rows, _ = lax.optimization_barrier((grad_attn_rows, new_down))
     grad_out_w = jnp.einsum("rd,rh->dh", grad_attn_rows, mixed_flat, preferred_element_type=f32)
     grad_mixed = jnp.dot(grad_attn_rows, output_full, preferred_element_type=f32).astype(bf16)
     grad_mixed = grad_mixed.reshape(seq_here, seq_len, kv_here, group_size, HD)
@@ -305,6 +307,9 @@
     grad_normed_one = scatter_blocks(
         split_rows(grad_in_one.astype(bf16).reshape(seq_here, seq_len, model_width))
     )
+    grad_gateup_s = jnp.stack([grad_gate_s, grad_up_s]).astype(f32)
+    new_gateup = adamw(w_gateup, grad_gateup_s, m_gateup, s_gateup, weight_decay)
+    grad_normed_one, _ = lax.optimization_barrier((grad_normed_one, new_gateup))
     scaled_one = attn_gain * grad_normed_one
     gain_one_part = jnp.sum(grad_normed_one * x_float * inv_one, axis=(0, 1))
     input_grad = (
@@ -315,9 +320,6 @@
     gain_grads = sum_everywhere(jnp.stack([gain_one_part, gain_two_part]))
     attn_send = jnp.concatenate([grad_qkv_w.astype(bf16), grad_out_w.astype(bf16)], axis=1)
     grad_attn_s = lax.psum_scatter(attn_send, "dp", scatter_dimension=0, tiled=True).astype(f32)
-    grad_down_s = grad_down_s.astype(f32)
-    grad_gate_s = grad_gate_s.astype(f32)
-    grad_up_s = grad_up_s.astype(f32)
     grads_all = (
         gain_grads[0],
         gain_grads[1],
@@ -326,17 +328,17 @@
             [grad_attn_s[:, q_cols : q_cols + kv_cols], grad_attn_s[:, q_cols + kv_cols : qkv_cols]]
         ),
         grad_attn_s[:, qkv_cols:].T,
-        jnp.stack([grad_gate_s, grad_up_s]),
-        grad_down_s,
-    )
-    params = (attn_gain, mlp_gain, w_query, w_keyval, w_output, w_gateup, w_down)
-    firsts = (m_attn_gain, m_mlp_gain, m_query, m_keyval, m_output, m_gateup, m_down)
-    seconds = (s_attn_gain, s_mlp_gain, s_query, s_keyval, s_output, s_gateup, s_down)
-    decays = (0.0, 0.0, weight_decay, weight_decay, weight_decay, weight_decay, weight_decay)
+        grad_gateup_s,
+        grad_down_s.astype(f32),
+    )
+    params = (attn_gain, mlp_gain, w_query, w_keyval, w_output)
+    firsts = (m_attn_gain, m_mlp_gain, m_query, m_keyval, m_output)
+    seconds = (s_attn_gain, s_mlp_gain, s_query, s_keyval, s_output)
+    decays = (0.0, 0.0, weight_decay, weight_decay, weight_decay)
     updated = [
         adamw(params[idx], grads_all[idx], firsts[idx], seconds[idx], decays[idx])
-        for idx in range(7)
-    ]
+        for idx in range(5)
+    ] + [new_gateup, new_down]
     return (
         block_out,
         input_grad,

time: 714 us -> 716 us (level)
    dot_general x2, matrix products: 11.4 us -> 4.22 us  [attend_back(): jnp.einsum('kgqs,qkgd->skd', probs_b, grad_mixed, preferred_element_type=...]
    unnamed x192 -> x180, local copies, waits for them, and re-layouts: 24.4 us -> 27.7 us
  transfers between devices with their start and end apart: 36 -> 36, of which waited for: 17 -> 16; matrix products, arithmetic and copies ran while one was open for 42% -> 42% of each run, Pallas kernels for 0% -> 0%
where the time goes in v1:
time: 716 us; the launch traced here: 710 us
  waiting for transfers between devices  330 us (46%)
  matrix products  188 us (26%)
  other arithmetic  91.2 us (13%)
  local copies, waits for them, and re-layouts  50.8 us (7%)
  starting transfers between devices  34.9 us (5%)
  between operations  15.7 us (2%)
    ppermute x12, waiting for transfers between devices, gather_blocks(): lax.ppermute(piece, 'tensor', swap_pairs(size, step))  166 us
    ppermute x12, waiting for transfers between devices, scatter_blocks(): lax.ppermute(blocks[step], 'tensor', swap_pairs(size, step))  150 us
    unnamed x180, local copies, waits for them, and re-layouts  27.7 us
    mul x7, other arithmetic, adamw(): return (-learn_rate * (update + decay * weight), first_new, second_new)  27.5 us
    dot_general x1, matrix products, body(): jnp.einsum('rd,fd->rf', grad_rows_late, down_full, preferred_element_type...  20.8 us
    dot_general x1, matrix products, body(): up_proj = jnp.dot(mlp_in, gateup_full[1], preferred_element_type=f32)  18 us
    convert_element_type x1, other arithmetic, attend_back(): grad_scores = (attn_probs * (grad_probs - row_delta)).astype(jnp.bfloat16)  15.7 us
    ppermute x12, starting transfers between devices, gather_blocks(): lax.ppermute(piece, 'tensor', swap_pairs(size, step))  15.5 us
  transfers between devices with their start and end apart: 36, of which 16 were waited for; matrix products, arithmetic and copies ran while one was open for 42% of the time, Pallas kernels for 0%

profile of v1, /device:TPU:0, one launch (start us, length us, event | category | flops | bytes accessed | tf_op | source)
XLA Modules:
  0.0 710.3 jit_solution(9685094464742409823)
XLA Ops:
  27.1 18.9 %collective-permute-done = bf16[2,128,2048]{2,1,0:T(8,128)(2,1)} collective-permute-done((bf16[2,128,2048]{2,1,0:T(8,128)(2,1)}, bf16[2,128,2048]{2,1,0:T(8,128)(2,1)}, u32[]{:S(2)}, u32[]{:S(2)}) %collective-permute-start) | collective-permute-done | bytes 1048608 | tf_op jit(solution)/shard_map/ppermute | solution.py:60
  46.0 23.1 %collective-permute-done.1 = bf16[2,128,2048]{2,1,0:T(8,128)(2,1)} collective-permute-done((bf16[2,128,2048]{2,1,0:T(8,128)(2,1)}, bf16[2,128,2048]{2,1,0:T(8,128)(2,1)}, u32[]{:S(2)}, u32[]{:S(2)}) %collective-permute-start.1) | collective-permute-done | bytes 1048608 | tf_op jit(solution)/shard_map/ppermute | solution.py:60
  119.8 19.5 %collective-permute-done.3 = bf16[2,128,2048]{2,1,0:T(8,128)(2,1)S(1)} collective-permute-done((bf16[2,128,2048]{2,1,0:T(8,128)(2,1)S(1)}, bf16[2,128,2048]{2,1,0:T(8,128)(2,1)S(1)}, u32[]{:S(2)}, u32[]{:S(2)}) %collective-permute-start.3) | collective-permute-done | bytes 1048608 | tf_op jit(solution)/shard_map/ppermute | solution.py:68
  141.0 22.2 %collective-permute-done.4 = bf16[2,128,2048]{2,1,0:T(8,128)(2,1)S(1)} collective-permute-done((bf16[2,128,2048]{2,1,0:T(8,128)(2,1)S(1)}, bf16[2,128,2048]{2,1,0:T(8,128)(2,1)S(1)}, u32[]{:S(2)}, u32[]{:S(2)}) %collective-permute-start.4) | collective-permute-done | bytes 1048608 | tf_op jit(solution)/shard_map/ppermute | solution.py:68
  167.8 16.5 %collective-permute-done.6 = bf16[2,128,2048]{2,1,0:T(8,128)(2,1)S(1)} collective-permute-done((bf16[2,128,2048]{2,1,0:T(8,128)(2,1)S(1)}, bf16[2,128,2048]{2,1,0:T(8,128)(2,1)S(1)}, u32[]{:S(2)}, u32[]{:S(2)}) %collective-permute-start.6) | collective-permute-done | bytes 1048608 | tf_op jit(solution)/shard_map/ppermute | solution.py:60
  185.7 44.9 %collective-permute-done.7 = bf16[2,128,2048]{2,1,0:T(8,128)(2,1)S(1)} collective-permute-done((bf16[2,128,2048]{2,1,0:T(8,128)(2,1)S(1)}, bf16[2,128,2048]{2,1,0:T(8,128)(2,1)S(1)}, u32[]{:S(2)}, u32[]{:S(2)}) %collective-permute-start.7) | collective-permute-done | bytes 1048608 | tf_op jit(solution)/shard_map/ppermute | solution.py:60
  232.9 18.4 %collective-permute-done.10 = bf16[2,128,2048]{2,1,0:T(8,128)(2,1)S(1)} collective-permute-done((bf16[2,128,2048]{2,1,0:T(8,128)(2,1)S(1)}, bf16[2,128,2048]{2,1,0:T(8,128)(2,1)S(1)}, u32[]{:S(2)}, u32[]{:S(2)}) %collective-permute-start.10) | collective-permute-done | bytes 1048608 | tf_op jit(solution)/shard_map/ppermute | solution.py:60
  253.6 13.5 %fusion.14 = f32[1024,2048]{1,0:T(8,128)S(1)} fusion(bf16[1024,2048]{1,0:T(8,128)(2,1)} %bitcast.281, bf16[2,2048,2048]{2,1,0:T(8,128)(2,1)} %all-gather.6.cloned.1.call-done), kind=kOutput, calls=%fused_computation.34 | convolution fusion | flops 8589934592 | bytes 20971520 | tf_op jit(solution)/shard_map/dot_general | solution.py:236
  267.1 18.0 %multiply_convert_fusion.2 = (bf16[1024,2048]{1,0:T(8,128)(2,1)}, f32[1024,2048]{1,0:T(8,128)}) fusion(f32[1024,2048]{1,0:T(8,128)S(1)} %fusion.14, bf16[1024,2048]{1,0:T(8,128)(2,1)S(1)} %bitcast.283, bf16[2,2048,2048]{2,1,0:T(8,128)(2,1)} %all-gather.6.cloned.1.call-done), kind=kOutput, calls=%fused_computation.23 | convolution fusion | flops 8602517504 | bytes 33554432 | tf_op jit(solution)/shard_map/dot_general | solution.py:237
  285.1 13.4 %convolution_convert_fusion.2 = bf16[2048,2048]{1,0:T(8,128)(2,1)} fusion(bf16[1024,2048]{1,0:T(8,128)(2,1)} %get-tuple-element.224, bf16[1024,2048]{1,0:T(8,128)(2,1)S(1)} %bitcast.290), kind=kOutput, calls=%fused_computation.32 | convolution fusion | flops 8594128896 | bytes 16777216 | tf_op jit(solution)/shard_map/rf,rd->fd/dot_general | solution.py:245
  306.3 20.8 %multiply_convert_fusion = (bf16[1024,2048]{1,0:T(8,128)(2,1)S(1)}, bf16[1024,2048]{1,0:T(8,128)(2,1)}) fusion(f32[1024,2048]{1,0:T(8,128)} %copy-done.75, f32[1024,2048]{1,0:T(8,128)} %get-tuple-element.225, bf16[1024,2048]{1,0:T(8,128)(2,1)} %bitcast.289, bf16[2048,2048]{1,0:T(8,128)(2,1)} %all-gather.8.cloned.1.call-done), kind=kOutput, calls=%fused_computation.21 | convolution fusion | flops 8617197568 | bytes 37748736 | tf_op jit(solution)/shard_map/rd,fd->rf/dot_general | solution.py:250
  327.0 12.6 %fusion.13 = f32[1024,2048]{1,0:T(8,128)S(1)} fusion(bf16[1024,2048]{1,0:T(8,128)(2,1)} %get-tuple-element.165, bf16[2,2048,2048]{2,1,0:T(8,128)(2,1)} %all-gather.6.cloned.1.call-done), kind=kOutput, calls=%fused_computation.33 | convolution fusion | flops 8589934592 | bytes 20971520 | tf_op jit(solution)/shard_map/rf,df->rd/dot_general | solution.py:255
  339.7 13.2 %add_convert_fusion = bf16[1024,2048]{1,0:T(8,128)(2,1)} fusion(f32[1024,2048]{1,0:T(8,128)S(1)} %fusion.13, bf16[1024,2048]{1,0:T(8,128)(2,1)S(1)} %get-tuple-element.164, bf16[2,2048,2048]{2,1,0:T(8,128)(2,1)} %all-gather.6.cloned.1.call-done), kind=kOutput, calls=%fused_computation.20 | convolution fusion | flops 8594128896 | bytes 25165824 | tf_op jit(solution)/shard_map/rf,df->rd/dot_general | solution.py:257
  352.9 11.5 %convolution_convert_fusion = bf16[2048,2048]{1,0:T(8,128)(2,1)} fusion(bf16[1024,2048]{1,0:T(8,128)(2,1)S(1)} %bitcast.284, bf16[1024,2048]{1,0:T(8,128)(2,1)S(1)} %get-tuple-element.164), kind=kOutput, calls=%fused_computation.30 | convolution fusion | flops 8594128896 | bytes 16777216 | tf_op jit(solution)/shard_map/rd,rf->df/dot_general | solution.py:266
  364.5 14.5 %convolution_convert_fusion.1 = bf16[2048,2048]{1,0:T(8,128)(2,1)} fusion(bf16[1024,2048]{1,0:T(8,128)(2,1)} %bitcast.282, bf16[1024,2048]{1,0:T(8,128)(2,1)} %get-tuple-element.165), kind=kOutput, calls=%fused_computation.31 | convolution fusion | flops 8594128896 | bytes 16777216 | tf_op jit(solution)/shard_map/rd,rf->df/dot_general | solution.py:263
  385.0 22.5 %collective-permute-done.12 = bf16[2,128,2048]{2,1,0:T(8,128)(2,1)S(1)} collective-permute-done((bf16[2,128,2048]{2,1,0:T(8,128)(2,1)S(1)}, bf16[2,128,2048]{2,1,0:T(8,128)(2,1)S(1)}, u32[]{:S(2)}, u32[]{:S(2)}) %collective-permute-start.12) | collective-permute-done | bytes 1048608 | tf_op jit(solution)/shard_map/ppermute | solution.py:68
  407.5 23.1 %collective-permute-done.13 = bf16[2,128,2048]{2,1,0:T(8,128)(2,1)S(1)} collective-permute-done((bf16[2,128,2048]{2,1,0:T(8,128)(2,1)S(1)}, bf16[2,128,2048]{2,1,0:T(8,128)(2,1)S(1)}, u32[]{:S(2)}, u32[]{:S(2)}) %collective-permute-start.13) | collective-permute-done | bytes 1048608 | tf_op jit(solution)/shard_map/ppermute | solution.py:68
  437.5 22.5 %collective-permute-done.15 = bf16[2,128,2048]{2,1,0:T(8,128)(2,1)S(1)} collective-permute-done((bf16[2,128,2048]{2,1,0:T(8,128)(2,1)S(1)}, bf16[2,128,2048]{2,1,0:T(8,128)(2,1)S(1)}, u32[]{:S(2)}, u32[]{:S(2)}) %collective-permute-start.15) | collective-permute-done | bytes 1048608 | tf_op jit(solution)/shard_map/ppermute | solution.py:60
  460.1 22.1 %collective-permute-done.16 = bf16[2,128,2048]{2,1,0:T(8,128)(2,1)S(1)} collective-permute-done((bf16[2,128,2048]{2,1,0:T(8,128)(2,1)S(1)}, bf16[2,128,2048]{2,1,0:T(8,128)(2,1)S(1)}, u32[]{:S(2)}, u32[]{:S(2)}) %collective-permute-start.16) | collective-permute-done | bytes 1048608 | tf_op jit(solution)/shard_map/ppermute | solution.py:60
  512.2 15.7 %fusion.2 = (bf16[2,4,512,512]{2,3,1,0:T(8,128)(2,1)S(1)}, bf16[2,4,512,512]{2,3,1,0:T(8,128)(2,1)}) fusion(f32[2,512,512,4]{2,1,3,0:T(8,128)} %get-tuple-element.227, f32[2,512,512,4]{2,1,3,0:T(8,128)} %copy-done.1, f32[2,4,512]{2,1,0:T(4,128)S(1)} %get-tuple-element.226, f32[2,4,512]{2,1,0:T(4,128)S(1)} %bitcast.321, pred[512,512]{0,1:T(8,128)(4,1)S(1)} %copy-done.14, ...), kind=kLoop, calls=%fused_computation.6 | loop fusion | flops 25165824 | bytes 42532864 | tf_op jit(solution)/shard_map/convert_element_type | solution.py:120
  547.9 12.8 %convolution_convert_fusion.3 = bf16[1024,2048]{1,0:T(8,128)(2,1)S(1)} fusion(bf16[1024,2048]{1,0:T(8,128)(2,1)} %get-tuple-element.224, bf16[2048,2048]{1,0:T(8,128)(2,1)} %all-gather.8.cloned.1.call-done), kind=kOutput, calls=%fused_computation.54 | convolution fusion | flops 8592031744 | bytes 16777216 | tf_op jit(solution)/shard_map/dot_general | solution.py:241
  577.8 11.2 %add_multiply_fusion = (f32[2,256,2048]{2,1,0:T(8,128)}, f32[2,256,2048]{2,1,0:T(8,128)}, f32[2,256,2048]{2,1,0:T(8,128)}, f32[2,256,2048]{2,1,0:T(8,128)}) fusion(f32[2,256,2048]{2,1,0:T(8,128)} %param.32, f32[2,256,2048]{2,1,0:T(8,128)} %param.39, f32[2,256,2048]{2,1,0:T(8,128)} %param.46, bf16[1,256,2048]{2,1,0:T(8,128)(2,1)} %bitcast.300, ...), kind=kLoop, calls=%fused_computation.52 | loop fusion | flops 16777216 | bytes 31457280 | tf_op jit(solution)/shard_map/mul | solution.py:141
  589.0 22.3 %collective-permute-done.21 = bf16[2,128,2048]{2,1,0:T(8,128)(2,1)} collective-permute-done((bf16[2,128,2048]{2,1,0:T(8,128)(2,1)}, bf16[2,128,2048]{2,1,0:T(8,128)(2,1)}, u32[]{:S(2)}, u32[]{:S(2)}) %collective-permute-start.21) | collective-permute-done | bytes 1048608 | tf_op jit(solution)/shard_map/ppermute | solution.py:68
  613.1 40.5 %collective-permute-done.22 = bf16[2,128,2048]{2,1,0:T(8,128)(2,1)} collective-permute-done((bf16[2,128,2048]{2,1,0:T(8,128)(2,1)}, bf16[2,128,2048]{2,1,0:T(8,128)(2,1)}, u32[]{:S(2)}, u32[]{:S(2)}) %collective-permute-start.22) | collective-permute-done | bytes 1048608 | tf_op jit(solution)/shard_map/ppermute | solution.py:68
  (349 shorter events, 220.8 us)
Async XLA Ops:
  7.2 65.7 %all-gather.4.cloned.1.call-start = ((), (), s32[]{:S(2)}) async-start(), calls=%async_computation.4 | async-start | bytes 5898240 | tf_op jit(solution)/shard_map/all_gather | solution.py:194
  12.5 241.1 %all-gather.6.cloned.1.call-start = ((), (), s32[]{:S(2)}) async-start(), calls=%async_computation.5 | async-start | bytes 18874368 | tf_op jit(solution)/shard_map/all_gather | solution.py:195
  16.5 289.7 %all-gather.8.cloned.1.call-start = ((), (), s32[]{:S(2)}) async-start(), calls=%async_computation.6 | async-start | bytes 9437184 | tf_op jit(solution)/shard_map/all_gather | solution.py:196
  21.7 47.4 %collective-permute-start.1 = (bf16[2,128,2048]{2,1,0:T(8,128)(2,1)}, bf16[2,128,2048]{2,1,0:T(8,128)(2,1)}, u32[]{:S(2)}, u32[]{:S(2)}) collective-permute-start(bf16[2,128,2048]{2,1,0:T(8,128)(2,1)} %fusion.26), channel_id=1, source_target_pairs={{0,2},{1,3},{2,0},{3,1},{4,6},{5,7},{6,4},{7,5},{8,10},{9,11},{10,... | collective-permute-start | bytes 3145736 | tf_op jit(solution)/shard_map/ppermute | solution.py:60
  24.3 460.3 %reduce-scatter.5.cloned.1.call-start = ((), (), s32[]{:S(2)}) async-start(), calls=%async_computation.7 | async-start | bytes 9437184 | tf_op jit(solution)/shard_map/reduce_scatter | solution.py:249
  114.7 48.5 %collective-permute-start.4 = (bf16[2,128,2048]{2,1,0:T(8,128)(2,1)S(1)}, bf16[2,128,2048]{2,1,0:T(8,128)(2,1)S(1)}, u32[]{:S(2)}, u32[]{:S(2)}) collective-permute-start(bf16[2,128,2048]{2,1,0:T(8,128)(2,1)S(1)} %get-tuple-element.177), channel_id=1, source_target_pairs={{0,2},{1,3},{2,0},{3,1},{4,6},{5,7},{6,4},{7,5},{8,10},{9,11},{10,... | collective-permute-start | bytes 3145736 | tf_op jit(solution)/shard_map/ppermute | solution.py:68
  115.5 47.7 %collective-permute-start.5 = (bf16[2,128,2048]{2,1,0:T(8,128)(2,1)S(1)}, bf16[2,128,2048]{2,1,0:T(8,128)(2,1)S(1)}, u32[]{:S(2)}, u32[]{:S(2)}) collective-permute-start(bf16[2,128,2048]{2,1,0:T(8,128)(2,1)S(1)} %get-tuple-element.176), channel_id=1, source_target_pairs={{0,3},{1,2},{2,1},{3,0},{4,7},{5,6},{6,5},{7,4},{8,11},{9,10},{10,... | collective-permute-start | bytes 3145736 | tf_op jit(solution)/shard_map/ppermute | solution.py:68
  117.5 66.8 %collective-permute-start.6 = (bf16[2,128,2048]{2,1,0:T(8,128)(2,1)S(1)}, bf16[2,128,2048]{2,1,0:T(8,128)(2,1)S(1)}, u32[]{:S(2)}, u32[]{:S(2)}) collective-permute-start(bf16[2,128,2048]{2,1,0:T(8,128)(2,1)S(1)} %broadcast_select_fusion), channel_id=1, source_target_pairs={{0,1},{1,0},{2,3},{3,2},{4,5},{5,4},{6,7},{7,6},{8,9},{9,8},{10,11... | collective-permute-start | bytes 3145736 | tf_op jit(solution)/shard_map/ppermute | solution.py:60
  119.0 111.6 %collective-permute-start.7 = (bf16[2,128,2048]{2,1,0:T(8,128)(2,1)S(1)}, bf16[2,128,2048]{2,1,0:T(8,128)(2,1)S(1)}, u32[]{:S(2)}, u32[]{:S(2)}) collective-permute-start(bf16[2,128,2048]{2,1,0:T(8,128)(2,1)S(1)} %broadcast_select_fusion), channel_id=1, source_target_pairs={{0,2},{1,3},{2,0},{3,1},{4,6},{5,7},{6,4},{7,5},{8,10},{9,11},{10,... | collective-permute-start | bytes 3145736 | tf_op jit(solution)/shard_map/ppermute | solution.py:60
  139.3 91.3 %collective-permute-start.8 = (bf16[2,128,2048]{2,1,0:T(8,128)(2,1)S(1)}, bf16[2,128,2048]{2,1,0:T(8,128)(2,1)S(1)}, u32[]{:S(2)}, u32[]{:S(2)}) collective-permute-start(bf16[2,128,2048]{2,1,0:T(8,128)(2,1)S(1)} %broadcast_select_fusion), channel_id=1, source_target_pairs={{0,3},{1,2},{2,1},{3,0},{4,7},{5,6},{6,5},{7,4},{8,11},{9,10},{10,... | collective-permute-start | bytes 3145736 | tf_op jit(solution)/shard_map/ppermute | solution.py:60
  165.6 85.7 %collective-permute-start.10 = (bf16[2,128,2048]{2,1,0:T(8,128)(2,1)S(1)}, bf16[2,128,2048]{2,1,0:T(8,128)(2,1)S(1)}, u32[]{:S(2)}, u32[]{:S(2)}) collective-permute-start(bf16[2,128,2048]{2,1,0:T(8,128)(2,1)S(1)} %multiply_convert_fusion.3), channel_id=1, source_target_pairs={{0,2},{1,3},{2,0},{3,1},{4,6},{5,7},{6,4},{7,5},{8,10},{9,11},{10,... | collective-permute-start | bytes 3145736 | tf_op jit(solution)/shard_map/ppermute | solution.py:60
  166.5 84.8 %collective-permute-start.11 = (bf16[2,128,2048]{2,1,0:T(8,128)(2,1)S(1)}, bf16[2,128,2048]{2,1,0:T(8,128)(2,1)S(1)}, u32[]{:S(2)}, u32[]{:S(2)}) collective-permute-start(bf16[2,128,2048]{2,1,0:T(8,128)(2,1)S(1)} %multiply_convert_fusion.3), channel_id=1, source_target_pairs={{0,3},{1,2},{2,1},{3,0},{4,7},{5,6},{6,5},{7,4},{8,11},{9,10},{10,... | collective-permute-start | bytes 3145736 | tf_op jit(solution)/shard_map/ppermute | solution.py:60
  184.3 67.0 %collective-permute-start.9 = (bf16[2,128,2048]{2,1,0:T(8,128)(2,1)S(1)}, bf16[2,128,2048]{2,1,0:T(8,128)(2,1)S(1)}, u32[]{:S(2)}, u32[]{:S(2)}) collective-permute-start(bf16[2,128,2048]{2,1,0:T(8,128)(2,1)S(1)} %multiply_convert_fusion.3), channel_id=1, source_target_pairs={{0,1},{1,0},{2,3},{3,2},{4,5},{5,4},{6,7},{7,6},{8,9},{9,8},{10,11... | collective-permute-start | bytes 3145736 | tf_op jit(solution)/shard_map/ppermute | solution.py:60
  306.2 271.5 %reduce-scatter.9.cloned.1.call-start = ((), (), s32[]{:S(2)}) async-start(), calls=%async_computation.9 | async-start | bytes 9437184 | tf_op jit(solution)/shard_map/reduce_scatter | solution.py:268
  364.5 213.3 %reduce-scatter.7.cloned.1.call-start = ((), (), s32[]{:S(2)}) async-start(), calls=%async_computation.8 | async-start | bytes 9437184 | tf_op jit(solution)/shard_map/reduce_scatter | solution.py:267
  379.1 304.7 %reduce-scatter.11.cloned.1.call-start = ((), (), s32[]{:S(2)}) async-start(), calls=%async_computation.10 | async-start | bytes 5898240 | tf_op jit(solution)/shard_map/reduce_scatter | solution.py:322
  382.9 47.7 %collective-permute-start.13 = (bf16[2,128,2048]{2,1,0:T(8,128)(2,1)S(1)}, bf16[2,128,2048]{2,1,0:T(8,128)(2,1)S(1)}, u32[]{:S(2)}, u32[]{:S(2)}) collective-permute-start(bf16[2,128,2048]{2,1,0:T(8,128)(2,1)S(1)} %get-tuple-element.174), channel_id=1, source_target_pairs={{0,2},{1,3},{2,0},{3,1},{4,6},{5,7},{6,4},{7,5},{8,10},{9,11},{10,... | collective-permute-start | bytes 3145736 | tf_op jit(solution)/shard_map/ppermute | solution.py:68
  384.3 46.2 %collective-permute-start.14 = (bf16[2,128,2048]{2,1,0:T(8,128)(2,1)S(1)}, bf16[2,128,2048]{2,1,0:T(8,128)(2,1)S(1)}, u32[]{:S(2)}, u32[]{:S(2)}) collective-permute-start(bf16[2,128,2048]{2,1,0:T(8,128)(2,1)S(1)} %get-tuple-element.173), channel_id=1, source_target_pairs={{0,3},{1,2},{2,1},{3,0},{4,7},{5,6},{6,5},{7,4},{8,11},{9,10},{10,... | collective-permute-start | bytes 3145736 | tf_op jit(solution)/shard_map/ppermute | solution.py:68
  435.2 47.0 %collective-permute-start.16 = (bf16[2,128,2048]{2,1,0:T(8,128)(2,1)S(1)}, bf16[2,128,2048]{2,1,0:T(8,128)(2,1)S(1)}, u32[]{:S(2)}, u32[]{:S(2)}) collective-permute-start(bf16[2,128,2048]{2,1,0:T(8,128)(2,1)S(1)} %fusion.74), channel_id=1, source_target_pairs={{0,2},{1,3},{2,0},{3,1},{4,6},{5,7},{6,4},{7,5},{8,10},{9,11},{10,... | collective-permute-start | bytes 3145736 | tf_op jit(solution)/shard_map/ppermute | solution.py:60
  562.4 107.1 %collective-permute-start.18 = (bf16[2,128,2048]{2,1,0:T(8,128)(2,1)}, bf16[2,128,2048]{2,1,0:T(8,128)(2,1)}, u32[]{:S(2)}, u32[]{:S(2)}) collective-permute-start(bf16[2,128,2048]{2,1,0:T(8,128)(2,1)} %get-tuple-element.169), channel_id=1, source_target_pairs={{0,1},{1,0},{2,3},{3,2},{4,5},{5,4},{6,7},{7,6},{8,9},{9,8},{10,11... | collective-permute-start | bytes 3145736 | tf_op jit(solution)/shard_map/ppermute | solution.py:68
  563.4 106.1 %collective-permute-start.19 = (bf16[2,128,2048]{2,1,0:T(8,128)(2,1)}, bf16[2,128,2048]{2,1,0:T(8,128)(2,1)}, u32[]{:S(2)}, u32[]{:S(2)}) collective-permute-start(bf16[2,128,2048]{2,1,0:T(8,128)(2,1)} %get-tuple-element.171), channel_id=1, source_target_pairs={{0,2},{1,3},{2,0},{3,1},{4,6},{5,7},{6,4},{7,5},{8,10},{9,11},{10,... | collective-permute-start | bytes 3145736 | tf_op jit(solution)/shard_map/ppermute | solution.py:68
  574.9 78.7 %collective-permute-start.22 = (bf16[2,128,2048]{2,1,0:T(8,128)(2,1)}, bf16[2,128,2048]{2,1,0:T(8,128)(2,1)}, u32[]{:S(2)}, u32[]{:S(2)}) collective-permute-start(bf16[2,128,2048]{2,1,0:T(8,128)(2,1)} %get-tuple-element.168), channel_id=1, source_target_pairs={{0,2},{1,3},{2,0},{3,1},{4,6},{5,7},{6,4},{7,5},{8,10},{9,11},{10,... | collective-permute-start | bytes 3145736 | tf_op jit(solution)/shard_map/ppermute | solution.py:68
  575.9 77.6 %collective-permute-start.23 = (bf16[2,128,2048]{2,1,0:T(8,128)(2,1)}, bf16[2,128,2048]{2,1,0:T(8,128)(2,1)}, u32[]{:S(2)}, u32[]{:S(2)}) collective-permute-start(bf16[2,128,2048]{2,1,0:T(8,128)(2,1)} %get-tuple-element.167), channel_id=1, source_target_pairs={{0,3},{1,2},{2,1},{3,0},{4,7},{5,6},{6,5},{7,4},{8,11},{9,10},{10,... | collective-permute-start | bytes 3145736 | tf_op jit(solution)/shard_map/ppermute | solution.py:68
  611.3 58.3 %collective-permute-start.20 = (bf16[2,128,2048]{2,1,0:T(8,128)(2,1)}, bf16[2,128,2048]{2,1,0:T(8,128)(2,1)}, u32[]{:S(2)}, u32[]{:S(2)}) collective-permute-start(bf16[2,128,2048]{2,1,0:T(8,128)(2,1)} %get-tuple-element.170), channel_id=1, source_target_pairs={{0,3},{1,2},{2,1},{3,0},{4,7},{5,6},{6,5},{7,4},{8,11},{9,10},{10,... | collective-permute-start | bytes 3145736 | tf_op jit(solution)/shard_map/ppermute | solution.py:68
  (92 other events, 1544.9 us)
Sparse Core Ops, SparseCore 0:
  12.6 59.1 all-gather.3
  74.0 149.2 all-gather.5
  225.5 80.6 all-gather.7
  308.3 87.6 reduce-scatter.4
  398.2 87.9 reduce-scatter.8
  488.4 87.9 reduce-scatter.6
  578.7 58.2 reduce-scatter.10
